TPU v7x, 512 devices: a whole 4x4x16 slice. The times are simulated.
512 devices in a mesh: dom: 32 (over x_hi, z), grp: 16 (over y, x_lo, core).
Axes of the slice: x: 4 (x_hi: 2, x_lo: 2; x = x_hi * 2 + x_lo), y: 4, z: 16, core: 2. Of those that a mesh axis runs over, the one named last changes fastest.
Arguments:
- adjoint_state: float32 [64, 16, 1024, 256], P('grp', None, 'dom'), may hold values from -6 to 6
- east_wind: float32 [16, 1024, 256], P(None, 'dom'), may hold values from -0.2 to 0.2
- north_wind: float32 [16, 1024, 256], P(None, 'dom'), may hold values from -0.2 to 0.2
- east_diff: float32 [16, 1024, 256], P(None, 'dom'), may hold values from 0.01 to 0.05
- north_diff: float32 [16, 1024, 256], P(None, 'dom'), may hold values from 0.01 to 0.05
- mass_flux: float32 [16, 1024, 256], P(None, 'dom'), may hold values from 0.05 to 0.45
- region_map: int32 [1024, 256], P('dom'), may hold values from 0 to 63
- cloud_top: int32 [1024, 256], P('dom'), may hold values from 1 to 15
Outputs:
- final_adjoint: float32 [64, 16, 1024, 256], P('grp', None, 'dom')
- flux_gradient: float32 [1024, 256], P('dom')
Inputs may be any that keep to these rules, and one draw needn't show every extreme that they name: `region_map`: tag k of the whole set of 64 tags belongs to region k.
All inputs are finite; a program needn't handle non-finite values.
Results may differ from a plain program's by a relative error of at most 0.00002.
Values sent between devices are 32-bit elements; how exact they have to be, the bound alone decides.
A program may use at most 64 MiB of HBM per device.

v0:
```python
import jax
import jax.numpy as jnp
from jax import lax
from jax.sharding import PartitionSpec as P

ITERS = 4


def passed_along(value, axis, by):
    size = lax.axis_size(axis)
    return lax.ppermute(value, axis, [(i, (i + by) % size) for i in range(size)])


def with_halo(cells, sides, width):
    for axis, dim in sides:
        count = lax.axis_size(axis)
        head = lax.slice_in_dim(cells, 0, width, axis=dim)
        tail = lax.slice_in_dim(cells, cells.shape[dim] - width, cells.shape[dim], axis=dim)
        cells = jnp.concatenate(
            [
                lax.ppermute(tail, axis, [(i, (i + 1) % count) for i in range(count)]),
                cells,
                lax.ppermute(head, axis, [((i + 1) % count, i) for i in range(count)]),
            ],
            axis=dim,
        )
    return cells


def local(
    adjoint_state, east_wind, north_wind, east_diff, north_diff, mass_flux, region_map, cloud_top
):
    tags, levels, cols, lats = adjoint_state.shape
    level_ids = lax.broadcasted_iota(jnp.int32, mass_flux.shape, 0)
    active = mass_flux * (level_ids < cloud_top[None]).astype(jnp.float32)
    stacked = jnp.stack([east_wind, east_diff, north_wind, north_diff, active])
    margin = 1
    edge = stacked[0:2, :, cols - 1 : cols]
    left_edge = passed_along(edge, "dom", 1)
    lower_rim = jnp.concatenate(
        [left_edge, jnp.zeros((3,) + left_edge.shape[1:], jnp.float32)], axis=0
    )
    padded = jnp.concatenate([lower_rim, stacked, jnp.zeros_like(lower_rim)], axis=2)
    wind_e = padded[0]
    diff_e = padded[1]
    wind_n = padded[2]
    diff_n = padded[3]
    updraft = padded[4]
    east_coef = jnp.maximum(wind_e, 0.0) + diff_e
    west_prime = jnp.maximum(-wind_e, 0.0) + diff_e
    row_ids = lax.broadcasted_iota(jnp.int32, wind_n.shape, 2)
    north_coef = (jnp.maximum(wind_n, 0.0) + diff_n) * (row_ids < lats - 1).astype(jnp.float32)
    south_prime = jnp.maximum(-wind_n, 0.0) + diff_n
    south_coef = jnp.concatenate(
        [jnp.zeros_like(south_prime[..., :1]), south_prime[..., :-1]], axis=-1
    )
    lam = adjoint_state
    accum = jnp.zeros((tags, cols, lats), jnp.float32)
    for round_step in range(ITERS // margin):
        current = with_halo(lam, (("dom", 2),), 1)
        center = current[:, :, 1 : 1 + cols]
        east = current[:, :, 2 : 2 + cols]
        west = current[:, :, 0:cols]
        coef_e = east_coef[:, margin : margin + cols]
        coef_w = west_prime[:, margin - 1 : margin - 1 + cols]
        coef_n = north_coef[:, margin : margin + cols]
        coef_s = south_coef[:, margin : margin + cols]
        lift = updraft[:, margin : margin + cols]
        north = jnp.concatenate([center[..., 1:], center[..., -1:]], axis=-1)
        south = jnp.concatenate([center[..., :1], center[..., :-1]], axis=-1)
        h = (
            center
            + coef_e * (east - center)
            + coef_w * (west - center)
            + coef_n * (north - center)
            + coef_s * (south - center)
        )
        above = jnp.concatenate([h[:, 1:], h[:, -1:]], axis=1)
        current = h + lift * (above - h)
        accum = accum + current[:, 0, 0:cols]
        lam = current
    tag_ids = lax.axis_index("grp") * tags + lax.broadcasted_iota(jnp.int32, (tags, cols, lats), 0)
    select = (region_map[None] == tag_ids).astype(jnp.float32)
    local_grad = jnp.sum(select * accum, axis=0)
    flux_gradient = lax.psum(local_grad, "grp")
    return (lam, flux_gradient)


def solution(mesh):
    return jax.shard_map(
        local,
        mesh=mesh,
        in_specs=(
            P("grp", None, "dom", None),
            P(None, "dom", None),
            P(None, "dom", None),
            P(None, "dom", None),
            P(None, "dom", None),
            P(None, "dom", None),
            P("dom", None),
            P("dom", None),
        ),
        out_specs=(P("grp", None, "dom", None), P("dom", None)),
        check_vma=False,
    )
```

profile of v0, /device:TPU:1, one launch (start us, length us, event | category | flops | bytes accessed | tf_op | source)
XLA Modules:
  0.0 144.0 jit_solution(17313663855327665156)
XLA Ops:
  0.6 1.2 pad_maximum_fusion.8
  1.8 4.4 %collective-permute-start = (f32[2,16,1,256]{3,2,1,0:T(1,128)S(1)}, f32[2,16,1,256]{3,2,1,0:T(1,128)S(1)}, u32[]{:S(2)}, u32[]{:S(2)}) collective-permute-start(f32[2,16,1,256]{3,2,1,0:T(1,128)S(1)} %pad_maximum_fusion.8), channel_id=1, source_target_pairs={{0,16},{16,32},{32,48},{48,64},{64,80},{80,96},{96,112},{112,128},... | collective-permute-start | bytes 98312 | tf_op jit(solution)/shard_map/ppermute | solution.py:11
  6.2 1.3 fusion.63
  7.5 12.0 %collective-permute-start.1 = (f32[4,16,1,256]{3,2,1,0:T(1,128)S(1)}, f32[4,16,1,256]{3,2,1,0:T(1,128)S(1)}, u32[]{:S(2)}, u32[]{:S(2)}) collective-permute-start(f32[4,16,1,256]{3,2,1,0:T(1,128)S(1)} %get-tuple-element.29), channel_id=1, source_target_pairs={{16,0},{32,16},{48,32},{64,48},{80,64},{96,80},{112,96},{128,112},... | collective-permute-start | bytes 196616 | tf_op jit(solution)/shard_map/ppermute | solution.py:23
  19.4 1.9 %collective-permute-start.2 = (f32[4,16,1,256]{3,2,1,0:T(1,128)S(1)}, f32[4,16,1,256]{3,2,1,0:T(1,128)S(1)}, u32[]{:S(2)}, u32[]{:S(2)}) collective-permute-start(f32[4,16,1,256]{3,2,1,0:T(1,128)S(1)} %get-tuple-element.30), channel_id=1, source_target_pairs={{0,16},{16,32},{32,48},{48,64},{64,80},{80,96},{96,112},{112,128},... | collective-permute-start | bytes 196616 | tf_op jit(solution)/shard_map/ppermute | solution.py:21
  21.4 1.9 %constant_dynamic-update-slice_fusion.1 = f32[5,16,32,256]{3,2,1,0:T(8,128)} fusion(f32[16,32,256]{2,1,0:T(8,128)} %param.9), kind=kLoop, calls=%fused_computation.90 | loop fusion | bytes 1048576
  23.3 2.8 %fusion.62 = (f32[4,16,32,255]{3,2,1,0:T(8,128)}, f32[4,16,32,255]{3,2,1,0:T(8,128)}) fusion(f32[4,16,32,256]{3,2,1,0:T(8,128)S(1)} %copy-done), kind=kLoop, calls=%fused_computation.103 | loop fusion | bytes 8355840 | tf_op jit(solution)/shard_map/slice | solution.py:70
  26.0 1.4 fusion.61
  27.4 0.8 constant_dynamic-update-slice_fusion
  28.3 1.9 %bitcast_dynamic-update-slice_fusion.2 = f32[5,16,32,256]{3,2,1,0:T(8,128)} fusion(f32[5,16,32,256]{3,2,1,0:T(8,128)} %constant_dynamic-update-slice_fusion, f32[16,32,256]{2,1,0:T(8,128)} %param.10), kind=kLoop, calls=%fused_computation.80 | loop fusion | bytes 1048576
  30.2 1.9 %bitcast_dynamic-update-slice_fusion.1 = f32[5,16,32,256]{3,2,1,0:T(8,128)} fusion(f32[5,16,32,256]{3,2,1,0:T(8,128)} %bitcast_dynamic-update-slice_fusion.2, f32[16,32,256]{2,1,0:T(8,128)} %param.12), kind=kLoop, calls=%fused_computation.79 | loop fusion | bytes 1048576
  32.0 1.9 %bitcast_dynamic-update-slice_fusion = f32[5,16,32,256]{3,2,1,0:T(8,128)} fusion(f32[5,16,32,256]{3,2,1,0:T(8,128)} %bitcast_dynamic-update-slice_fusion.1, f32[16,32,256]{2,1,0:T(8,128)} %param.13, s32[32,256]{1,0:T(8,128)S(1)} %copy-done.6), kind=kLoop, calls=%fused_computation.78 | loop fusion | flops 262144 | bytes 1081344 | tf_op jit(solution)/shard_map/stack | solution.py:36
  34.0 2.2 %fusion = f32[5,16,34,256]{3,2,1,0:T(8,128)S(1)} fusion(f32[2,16,1,256]{3,2,1,0:T(1,128)S(1)} %collective-permute-done, f32[5,16,32,256]{3,2,1,0:T(8,128)} %bitcast_dynamic-update-slice_fusion, f32[34]{0:T(128)S(1)} %pad.44.clone), kind=kLoop, calls=%fused_computation.1 | loop fusion | flops 2785280 | bytes 5439624 | tf_op jit(solution)/shard_map/concatenate | solution.py:43
  37.0 1.1 copy-done.2
  39.1 1.9 %fusion.29 = f32[4,16,32,256]{3,2,1,0:T(8,128)S(1)} fusion(f32[4,16,32,256]{3,2,1,0:T(8,128)S(1)} %copy-done, f32[4,16,1,256]{3,2,1,0:T(1,128)S(1)} %collective-permute-done.2, f32[4,16,1,256]{3,2,1,0:T(1,128)S(1)} %collective-permute-done.1, f32[4,16,32,1]{3,2,1,0:T(8,128)S(1)} %copy-done.3, f32[4,16,32,255]{3,2,1,0:T(8,128)S(1)} %copy-done.2, ...), kind=kLoop, calls=%fused_computation.38 | loop fusion | flops 8388608 | bytes 10616832 | tf_op jit(solution)/shard_map/add | solution.py:72
  41.3 0.7 fusion.36
  42.0 0.8 fusion.59
  42.9 7.0 %collective-permute-start.3 = (f32[4,16,1,256]{3,2,1,0:T(1,128)S(1)}, f32[4,16,1,256]{3,2,1,0:T(1,128)S(1)}, u32[]{:S(2)}, u32[]{:S(2)}) collective-permute-start(f32[4,16,1,256]{3,2,1,0:T(1,128)S(1)} %get-tuple-element.23), channel_id=1, source_target_pairs={{16,0},{32,16},{48,32},{64,48},{80,64},{96,80},{112,96},{128,112},... | collective-permute-start | bytes 196616 | tf_op jit(solution)/shard_map/ppermute | solution.py:23
  49.9 1.9 %collective-permute-start.4 = (f32[4,16,1,256]{3,2,1,0:T(1,128)S(1)}, f32[4,16,1,256]{3,2,1,0:T(1,128)S(1)}, u32[]{:S(2)}, u32[]{:S(2)}) collective-permute-start(f32[4,16,1,256]{3,2,1,0:T(1,128)S(1)} %get-tuple-element.24), channel_id=1, source_target_pairs={{0,16},{16,32},{32,48},{48,64},{64,80},{80,96},{96,112},{112,128},... | collective-permute-start | bytes 196616 | tf_op jit(solution)/shard_map/ppermute | solution.py:21
  52.2 6.3 %collective-permute-done.4 = f32[4,16,1,256]{3,2,1,0:T(1,128)S(1)} collective-permute-done((f32[4,16,1,256]{3,2,1,0:T(1,128)S(1)}, f32[4,16,1,256]{3,2,1,0:T(1,128)S(1)}, u32[]{:S(2)}, u32[]{:S(2)}) %collective-permute-start.4) | collective-permute-done | bytes 65568 | tf_op jit(solution)/shard_map/ppermute | solution.py:21
  58.5 2.0 %fusion.21 = f32[4,16,32,256]{3,2,1,0:T(8,128)S(1)} fusion(f32[4,16,32,256]{3,2,1,0:T(8,128)S(1)} %fusion.36, f32[4,16,1,256]{3,2,1,0:T(1,128)S(1)} %collective-permute-done.4, f32[4,16,1,256]{3,2,1,0:T(1,128)S(1)} %collective-permute-done.3, f32[4,16,32,1]{3,2,1,0:T(8,128)S(1)} %get-tuple-element.20, f32[4,16,32,255]{3,2,1,0:T(8,128)S(1)} %get-tuple-element.22, ...), kind=kLoop, calls=%fused_computation.28 | loop fusion | flops 8388608 | bytes 10616832 | tf_op jit(solution)/shard_map/add | solution.py:72
  61.5 0.8 fusion.56
  62.5 1.9 %collective-permute-start.5 = (f32[4,16,1,256]{3,2,1,0:T(1,128)S(1)}, f32[4,16,1,256]{3,2,1,0:T(1,128)S(1)}, u32[]{:S(2)}, u32[]{:S(2)}) collective-permute-start(f32[4,16,1,256]{3,2,1,0:T(1,128)S(1)} %get-tuple-element.17), channel_id=1, source_target_pairs={{16,0},{32,16},{48,32},{64,48},{80,64},{96,80},{112,96},{128,112},... | collective-permute-start | bytes 196616 | tf_op jit(solution)/shard_map/ppermute | solution.py:23
  64.4 3.4 %collective-permute-start.6 = (f32[4,16,1,256]{3,2,1,0:T(1,128)S(1)}, f32[4,16,1,256]{3,2,1,0:T(1,128)S(1)}, u32[]{:S(2)}, u32[]{:S(2)}) collective-permute-start(f32[4,16,1,256]{3,2,1,0:T(1,128)S(1)} %get-tuple-element.18), channel_id=1, source_target_pairs={{0,16},{16,32},{32,48},{48,64},{64,80},{80,96},{96,112},{112,128},... | collective-permute-start | bytes 196616 | tf_op jit(solution)/shard_map/ppermute | solution.py:21
  68.2 4.9 %collective-permute-done.6 = f32[4,16,1,256]{3,2,1,0:T(1,128)S(1)} collective-permute-done((f32[4,16,1,256]{3,2,1,0:T(1,128)S(1)}, f32[4,16,1,256]{3,2,1,0:T(1,128)S(1)}, u32[]{:S(2)}, u32[]{:S(2)}) %collective-permute-start.6) | collective-permute-done | bytes 65568 | tf_op jit(solution)/shard_map/ppermute | solution.py:21
  73.0 2.0 %fusion.13 = f32[4,16,32,256]{3,2,1,0:T(8,128)S(1)} fusion(f32[4,16,32,256]{3,2,1,0:T(8,128)S(1)} %fusion.40, f32[4,16,1,256]{3,2,1,0:T(1,128)S(1)} %collective-permute-done.6, f32[4,16,1,256]{3,2,1,0:T(1,128)S(1)} %collective-permute-done.5, f32[4,16,32,1]{3,2,1,0:T(8,128)S(1)} %get-tuple-element.14, f32[4,16,32,255]{3,2,1,0:T(8,128)S(1)} %get-tuple-element.16, ...), kind=kLoop, calls=%fused_computation.18 | loop fusion | flops 8388608 | bytes 10616832 | tf_op jit(solution)/shard_map/add | solution.py:72
  75.9 0.8 fusion.53
  76.8 1.9 %collective-permute-start.7 = (f32[4,16,1,256]{3,2,1,0:T(1,128)S(1)}, f32[4,16,1,256]{3,2,1,0:T(1,128)S(1)}, u32[]{:S(2)}, u32[]{:S(2)}) collective-permute-start(f32[4,16,1,256]{3,2,1,0:T(1,128)S(1)} %get-tuple-element.11), channel_id=1, source_target_pairs={{16,0},{32,16},{48,32},{64,48},{80,64},{96,80},{112,96},{128,112},... | collective-permute-start | bytes 196616 | tf_op jit(solution)/shard_map/ppermute | solution.py:23
  78.8 3.4 %collective-permute-start.8 = (f32[4,16,1,256]{3,2,1,0:T(1,128)S(1)}, f32[4,16,1,256]{3,2,1,0:T(1,128)S(1)}, u32[]{:S(2)}, u32[]{:S(2)}) collective-permute-start(f32[4,16,1,256]{3,2,1,0:T(1,128)S(1)} %get-tuple-element.12), channel_id=1, source_target_pairs={{0,16},{16,32},{32,48},{48,64},{64,80},{80,96},{96,112},{112,128},... | collective-permute-start | bytes 196616 | tf_op jit(solution)/shard_map/ppermute | solution.py:21
  82.5 4.9 %collective-permute-done.8 = f32[4,16,1,256]{3,2,1,0:T(1,128)S(1)} collective-permute-done((f32[4,16,1,256]{3,2,1,0:T(1,128)S(1)}, f32[4,16,1,256]{3,2,1,0:T(1,128)S(1)}, u32[]{:S(2)}, u32[]{:S(2)}) %collective-permute-start.8) | collective-permute-done | bytes 65568 | tf_op jit(solution)/shard_map/ppermute | solution.py:21
  87.4 2.0 %fusion.5 = f32[4,16,32,256]{3,2,1,0:T(8,128)S(1)} fusion(f32[4,16,32,256]{3,2,1,0:T(8,128)S(1)} %fusion.44, f32[4,16,1,256]{3,2,1,0:T(1,128)S(1)} %collective-permute-done.8, f32[4,16,1,256]{3,2,1,0:T(1,128)S(1)} %collective-permute-done.7, f32[4,16,32,1]{3,2,1,0:T(8,128)S(1)} %get-tuple-element.8, f32[4,16,32,255]{3,2,1,0:T(8,128)S(1)} %get-tuple-element.10, ...), kind=kLoop, calls=%fused_computation.8 | loop fusion | flops 8388608 | bytes 10616832 | tf_op jit(solution)/shard_map/add | solution.py:72
  90.5 53.5 %psum.7 = f32[32,256]{1,0:T(8,128)} all-reduce(f32[32,256]{1,0:T(8,128)S(1)} %fusion.51), channel_id=1, replica_groups=mesh['dom'=32,'grp'=16] {'grp'}, use_global_device_ids=true, to_apply=%region_1.0 | all-reduce | flops 8192 | bytes 65536 | tf_op jit(solution)/shard_map/psum | solution.py:85
  (47 shorter events, 6.2 us)
Async XLA Ops:
  0.6 22.6 %copy-start = (f32[4,16,32,256]{3,2,1,0:T(8,128)S(1)}, f32[4,16,32,256]{3,2,1,0:T(8,128)}, u32[]{:S(2)}) copy-start(f32[4,16,32,256]{3,2,1,0:T(8,128)} %param.8) | copy-start | bytes 6291460
  1.8 32.2 %collective-permute-start = (f32[2,16,1,256]{3,2,1,0:T(1,128)S(1)}, f32[2,16,1,256]{3,2,1,0:T(1,128)S(1)}, u32[]{:S(2)}, u32[]{:S(2)}) collective-permute-start(f32[2,16,1,256]{3,2,1,0:T(1,128)S(1)} %pad_maximum_fusion.8), channel_id=1, source_target_pairs={{0,16},{16,32},{32,48},{48,64},{64,80},{80,96},{96,112},{112,128},... | collective-permute-start | bytes 98312 | tf_op jit(solution)/shard_map/ppermute | solution.py:11
  7.5 29.5 %collective-permute-start.1 = (f32[4,16,1,256]{3,2,1,0:T(1,128)S(1)}, f32[4,16,1,256]{3,2,1,0:T(1,128)S(1)}, u32[]{:S(2)}, u32[]{:S(2)}) collective-permute-start(f32[4,16,1,256]{3,2,1,0:T(1,128)S(1)} %get-tuple-element.29), channel_id=1, source_target_pairs={{16,0},{32,16},{48,32},{64,48},{80,64},{96,80},{112,96},{128,112},... | collective-permute-start | bytes 196616 | tf_op jit(solution)/shard_map/ppermute | solution.py:23
  19.4 17.6 %collective-permute-start.2 = (f32[4,16,1,256]{3,2,1,0:T(1,128)S(1)}, f32[4,16,1,256]{3,2,1,0:T(1,128)S(1)}, u32[]{:S(2)}, u32[]{:S(2)}) collective-permute-start(f32[4,16,1,256]{3,2,1,0:T(1,128)S(1)} %get-tuple-element.30), channel_id=1, source_target_pairs={{0,16},{16,32},{32,48},{48,64},{64,80},{80,96},{96,112},{112,128},... | collective-permute-start | bytes 196616 | tf_op jit(solution)/shard_map/ppermute | solution.py:21
  26.0 1.4 copy-start.5
  27.4 4.6 %copy-start.6 = (s32[32,256]{1,0:T(8,128)S(1)}, s32[32,256]{1,0:T(8,128)}, u32[]{:S(2)}) copy-start(s32[32,256]{1,0:T(8,128)} %param.15) | copy-start | bytes 98308
  36.6 1.6 %copy-start.2 = (f32[4,16,32,255]{3,2,1,0:T(8,128)S(1)}, f32[4,16,32,255]{3,2,1,0:T(8,128)}, u32[]{:S(2)}) copy-start(f32[4,16,32,255]{3,2,1,0:T(8,128)} %get-tuple-element.28) | copy-start | bytes 6266884
  36.8 2.1 %copy-start.1 = (f32[4,16,32,255]{3,2,1,0:T(8,128)S(1)}, f32[4,16,32,255]{3,2,1,0:T(8,128)}, u32[]{:S(2)}) copy-start(f32[4,16,32,255]{3,2,1,0:T(8,128)} %get-tuple-element.27) | copy-start | bytes 6266884
  36.8 2.3 %copy-start.3 = (f32[4,16,32,1]{3,2,1,0:T(8,128)S(1)}, f32[4,16,32,1]{3,2,1,0:T(8,128)}, u32[]{:S(2)}) copy-start(f32[4,16,32,1]{3,2,1,0:T(8,128)} %get-tuple-element.26) | copy-start | bytes 24580
  42.9 9.3 %collective-permute-start.3 = (f32[4,16,1,256]{3,2,1,0:T(1,128)S(1)}, f32[4,16,1,256]{3,2,1,0:T(1,128)S(1)}, u32[]{:S(2)}, u32[]{:S(2)}) collective-permute-start(f32[4,16,1,256]{3,2,1,0:T(1,128)S(1)} %get-tuple-element.23), channel_id=1, source_target_pairs={{16,0},{32,16},{48,32},{64,48},{80,64},{96,80},{112,96},{128,112},... | collective-permute-start | bytes 196616 | tf_op jit(solution)/shard_map/ppermute | solution.py:23
  49.9 8.6 %collective-permute-start.4 = (f32[4,16,1,256]{3,2,1,0:T(1,128)S(1)}, f32[4,16,1,256]{3,2,1,0:T(1,128)S(1)}, u32[]{:S(2)}, u32[]{:S(2)}) collective-permute-start(f32[4,16,1,256]{3,2,1,0:T(1,128)S(1)} %get-tuple-element.24), channel_id=1, source_target_pairs={{0,16},{16,32},{32,48},{48,64},{64,80},{80,96},{96,112},{112,128},... | collective-permute-start | bytes 196616 | tf_op jit(solution)/shard_map/ppermute | solution.py:21
  62.5 5.7 %collective-permute-start.5 = (f32[4,16,1,256]{3,2,1,0:T(1,128)S(1)}, f32[4,16,1,256]{3,2,1,0:T(1,128)S(1)}, u32[]{:S(2)}, u32[]{:S(2)}) collective-permute-start(f32[4,16,1,256]{3,2,1,0:T(1,128)S(1)} %get-tuple-element.17), channel_id=1, source_target_pairs={{16,0},{32,16},{48,32},{64,48},{80,64},{96,80},{112,96},{128,112},... | collective-permute-start | bytes 196616 | tf_op jit(solution)/shard_map/ppermute | solution.py:23
  64.4 8.6 %collective-permute-start.6 = (f32[4,16,1,256]{3,2,1,0:T(1,128)S(1)}, f32[4,16,1,256]{3,2,1,0:T(1,128)S(1)}, u32[]{:S(2)}, u32[]{:S(2)}) collective-permute-start(f32[4,16,1,256]{3,2,1,0:T(1,128)S(1)} %get-tuple-element.18), channel_id=1, source_target_pairs={{0,16},{16,32},{32,48},{48,64},{64,80},{80,96},{96,112},{112,128},... | collective-permute-start | bytes 196616 | tf_op jit(solution)/shard_map/ppermute | solution.py:21
  76.8 5.7 %collective-permute-start.7 = (f32[4,16,1,256]{3,2,1,0:T(1,128)S(1)}, f32[4,16,1,256]{3,2,1,0:T(1,128)S(1)}, u32[]{:S(2)}, u32[]{:S(2)}) collective-permute-start(f32[4,16,1,256]{3,2,1,0:T(1,128)S(1)} %get-tuple-element.11), channel_id=1, source_target_pairs={{16,0},{32,16},{48,32},{64,48},{80,64},{96,80},{112,96},{128,112},... | collective-permute-start | bytes 196616 | tf_op jit(solution)/shard_map/ppermute | solution.py:23
  78.8 8.6 %collective-permute-start.8 = (f32[4,16,1,256]{3,2,1,0:T(1,128)S(1)}, f32[4,16,1,256]{3,2,1,0:T(1,128)S(1)}, u32[]{:S(2)}, u32[]{:S(2)}) collective-permute-start(f32[4,16,1,256]{3,2,1,0:T(1,128)S(1)} %get-tuple-element.12), channel_id=1, source_target_pairs={{0,16},{16,32},{32,48},{48,64},{64,80},{80,96},{96,112},{112,128},... | collective-permute-start | bytes 196616 | tf_op jit(solution)/shard_map/ppermute | solution.py:21
  89.7 0.8 copy-start.7
  90.4 53.6 %copy-start.4 = (f32[4,16,32,256]{3,2,1,0:T(8,128)}, f32[4,16,32,256]{3,2,1,0:T(8,128)S(1)}, u32[]{:S(2)}) copy-start(f32[4,16,32,256]{3,2,1,0:T(8,128)S(1)} %fusion.48) | copy-start | bytes 6291460
where the time goes:
time: 146 us; the launch traced here: 144 us
  blocking collectives  53.5 us (37%)
  starting transfers between devices  37.7 us (26%)
  local copies, waits for them, and re-layouts  19.3 us (13%)
  other arithmetic  16.4 us (11%)
  waiting for transfers between devices  16.1 us (11%)
    psum x1, blocking collectives, local(): flux_gradient = lax.psum(local_grad, 'grp')  53.5 us
    ppermute x4, starting transfers between devices, with_halo(): lax.ppermute(head, axis, [((i + 1) % count, i) for i in range(count)])  22.8 us
    ppermute x4, waiting for transfers between devices, with_halo(): lax.ppermute(tail, axis, [(i, (i + 1) % count) for i in range(count)])  16 us
    ppermute x4, starting transfers between devices, with_halo(): lax.ppermute(tail, axis, [(i, (i + 1) % count) for i in range(count)])  10.6 us
    unnamed x20, local copies, waits for them, and re-layouts  8.83 us
    add x4, other arithmetic, local(): center + coef_e * (east - center) + coef_w * (west - center)  8 us
    slice x8, local copies, waits for them, and re-layouts, local(): south = jnp.concatenate([center[..., :1], center[..., :-1]], axis=-1)  7.72 us
    ppermute x1, starting transfers between devices, passed_along(): lax.ppermute(value, axis, [(i, (i + by) % size) for i in range(size)])  4.38 us
  transfers between devices with their start and end apart: 9, of which 3 were waited for; matrix products, arithmetic and copies ran while one was open for 12% of the time, Pallas kernels for 0%

commit v1 on v0

v1 whole, which is shorter than its diff:
```python
import jax
import jax.numpy as jnp
from jax import lax
from jax.experimental import pallas as pl
from jax.experimental.pallas import tpu as pltpu
from jax.sharding import PartitionSpec as P

ITERS = 4
MESH = pl.DeviceIdType.MESH
CE, CW, CN, CS, C0, UP = range(6)


def turned(value):
    return jnp.swapaxes(value, 0, 1)


def kernel(
    x_ref, ew_ref, nw_ref, ed_ref, nd_ref, mf_ref, reg_ref, top_ref,
    lam_ref, grad_ref,
    raw, wraw, state, coef, ctop, regs, halo, whalo, thalo, save_l, save_r, west_end,
    acc, part1, part2, got1, got2,
    in_sem, xs_sem, xr_sem, ws_sem, wr_sem, fs_sem, fr_sem, g1s, g1r, g2s, g2r,
):
    tags, levels, cols, lats = x_ref.shape
    groups = lax.axis_size("grp")
    count = lax.axis_size("dom")
    me = lax.axis_index("dom")
    grp = lax.axis_index("grp")
    east_dev = lax.rem(me + 1, count)
    west_dev = lax.rem(me + count - 1, count)
    half = lax.rem(grp, 2)
    twin = grp + 1 - 2 * half
    H = ITERS
    hl = levels // 2

    winds = (ew_ref, ed_ref, nw_ref, nd_ref, mf_ref)
    barrier = pltpu.get_barrier_semaphore()
    for q in (east_dev, west_dev):
        pl.semaphore_signal(barrier, inc=1, device_id={"dom": q}, device_id_type=MESH)
    for d in range(1, groups):
        pl.semaphore_signal(
            barrier, inc=1, device_id={"grp": lax.rem(grp + d, groups)}, device_id_type=MESH
        )
    loads = [pltpu.make_async_copy(w, wraw.at[a], in_sem.at[a]) for a, w in enumerate(winds)]
    loads.append(pltpu.make_async_copy(top_ref, ctop, in_sem.at[5]))
    loads.append(pltpu.make_async_copy(reg_ref, regs, in_sem.at[6]))
    loads.append(pltpu.make_async_copy(x_ref, raw, in_sem.at[7]))
    for c in loads:
        c.start()

    lane = lax.broadcasted_iota(jnp.int32, (8, levels, lats), 2)
    level = lax.broadcasted_iota(jnp.int32, (levels, 8, lats), 0)

    def derive(ew, ed, nw, nd, mf, top, before):
        lift = mf * (level < jnp.minimum(top, levels - 1)[None]).astype(jnp.float32)
        ew, ed, nw, nd, lift = turned(ew), turned(ed), turned(nw), turned(nd), turned(lift)
        east = jnp.maximum(ew, 0.0) + ed
        prime = jnp.maximum(-ew, 0.0) + ed
        west = jnp.concatenate([before[None], prime[:-1]], axis=0)
        north = jnp.where(lane < lats - 1, jnp.maximum(nw, 0.0) + nd, 0.0)
        south = jnp.where(lane > 0, pltpu.roll(jnp.maximum(-nw, 0.0) + nd, 1, 2), 0.0)
        keep = 1.0 - east - west - north - south
        return (east, west, north, south, keep, lift), prime

    for c in loads[:6]:
        c.wait()

    def derive_tile(i, before):
        at = pl.ds(pl.multiple_of(8 * i, 8), 8)
        made, prime = derive(*[wraw[a, :, at, :] for a in range(5)], ctop[at, :], before)
        for m in range(6):
            coef[m, pl.ds(H + 8 * i, 8)] = made[m]
        return prime[7]

    west_end[...] = lax.fori_loop(
        0, cols // 8, derive_tile, jnp.zeros((levels, lats), jnp.float32)
    )

    loads[7].wait()
    loads[6].wait()

    @pl.loop(0, tags)
    def _(k):
        for i in range(cols // 8):
            state[k, pl.ds(H + 8 * i, 8)] = turned(raw[k, :, 8 * i : 8 * i + 8, :])

    pl.semaphore_wait(barrier, groups + 1)

    mine = pl.ds(pl.multiple_of(half * hl, hl), hl)
    sends = []
    sides = ((0, east_dev, cols - H, 0), (1, west_dev, 0, H))
    for s, q, src, dst in sides:
        for a, w in enumerate(winds):
            sends.append(
                pltpu.make_async_remote_copy(
                    w.at[mine, src : src + H, :],
                    whalo.at[a, mine, dst : dst + H, :],
                    ws_sem.at[s, a], wr_sem.at[s, a],
                    device_id={"dom": q}, device_id_type=MESH,
                )
            )
        sends.append(
            pltpu.make_async_remote_copy(
                top_ref.at[src : src + H, :], thalo.at[dst : dst + H, :],
                ws_sem.at[s, 5], wr_sem.at[s, 5],
                device_id={"dom": q}, device_id_type=MESH,
            )
        )
    for c in sends:
        c.start()
    xsends = []
    for p in range(tags // 2):
        for s, q, src, dst in sides:
            c = pltpu.make_async_remote_copy(
                x_ref.at[2 * p : 2 * p + 2, :, src : src + H, :],
                halo.at[2 * p : 2 * p + 2, :, dst : dst + H, :],
                xs_sem.at[s, p], xr_sem.at[s, p],
                device_id={"dom": q}, device_id_type=MESH,
            )
            c.start()
            xsends.append(c)

    def advance(left, cen, right, c):
        north = pltpu.roll(cen, lats - 1, 2)
        south = pltpu.roll(cen, 1, 2)
        h = (
            coef[C0, c][None] * cen
            + coef[CE, c][None] * right
            + coef[CW, c][None] * left
            + coef[CN, c][None] * north
            + coef[CS, c][None] * south
        )
        above = pltpu.roll(h, levels - 1, 1)
        return h + coef[UP, c][None] * (above - h)

    acc[...] = jnp.zeros_like(acc)

    @pl.loop(0, tags // 2)
    def _(p):
        ks = pl.ds(2 * p, 2)

        @pl.loop(1, ITERS + 1)
        def _(t):
            left = state[ks, H + t - 1]
            cen = state[ks, H + t]
            save_l[ks, t - 1] = cen

            def body(c, carry):
                left, cen = carry
                right = state[ks, c + 1]
                new = advance(left, cen, right, c)
                state[ks, c] = new
                acc[ks, c] += new[:, 0:8]
                return cen, right

            left, cen = lax.fori_loop(H + t, H + cols - t, body, (left, cen))
            save_r[ks, t - 1] = left

    tag0 = grp * tags
    row = lax.broadcasted_iota(jnp.int32, (8, lats), 0)

    for i in range(cols // 8):
        here = regs[8 * i : 8 * i + 8, :]
        total = jnp.zeros((8, lats), jnp.float32)
        for k in range(tags):
            top = turned(acc[k, H + 8 * i : H + 8 * i + 8])[0]
            total += jnp.where(here == tag0 + k, top, 0.0)
        part1[8 * i : 8 * i + 8, :] = total

    def spread(part, got, ss, rs):
        out = []
        for d in range(1, groups):
            c = pltpu.make_async_remote_copy(
                part, got.at[d - 1], ss.at[d - 1], rs.at[d - 1],
                device_id={"grp": lax.rem(grp + d, groups)}, device_id_type=MESH,
            )
            c.start()
            out.append(c)
        return out

    early = spread(part1, got1, g1s, g1r)

    @pl.loop(0, tags)
    def _(k):
        for s in (0, H + cols - 4):
            acc[k, s : s + 8] = jnp.zeros((8, 8, lats), jnp.float32)
        for i in range(1, cols // 8 - 1):
            lam_ref[k, :, 8 * i : 8 * i + 8, :] = turned(state[k, H + 8 * i : H + 8 * i + 8])

    for c in sends:
        c.wait_recv()
    share = pltpu.make_async_remote_copy(
        whalo.at[:, mine], whalo.at[:, mine], fs_sem, fr_sem,
        device_id={"grp": twin}, device_id_type=MESH,
    )
    share.start()
    share.wait_recv()

    made, prime = derive(*[whalo[a] for a in range(5)], thalo[...], jnp.zeros((levels, lats), jnp.float32))
    for m in range(6):
        coef[m, 0:H] = made[m][0:H]
        coef[m, H + cols : 2 * H + cols] = made[m][H:]
    first = prime[H - 1]
    coef[CW, H] = first
    coef[C0, H] = coef[C0, H] - first
    last = west_end[...]
    coef[CW, H + cols] = last
    coef[C0, H + cols] = made[C0][H] + made[CW][H] - last

    for p in range(tags // 2):
        for c in xsends[2 * p : 2 * p + 2]:
            c.wait_recv()
        for k in (2 * p, 2 * p + 1):
            edge = turned(halo[k])
            state[k, 0:H] = edge[0:H]
            state[k, H + cols : 2 * H + cols] = edge[H:]
        ks = pl.ds(2 * p, 2)

        @pl.loop(1, ITERS + 1)
        def _(t):
            left, cen = state[ks, t - 1], state[ks, t]
            for n in range(H):
                right = state[ks, t + n + 1] if n < H - 1 else save_l[ks, t - 1]
                new = advance(left, cen, right, t + n)
                state[ks, t + n] = new
                acc[ks, t + n] += new[:, 0:8]
                left, cen = cen, right
            base = H + cols - t
            left, cen = save_r[ks, t - 1], state[ks, base]
            for n in range(H):
                right = state[ks, base + n + 1]
                new = advance(left, cen, right, base + n)
                state[ks, base + n] = new
                acc[ks, base + n] += new[:, 0:8]
                left, cen = cen, right

    here = jnp.where(row < H, regs[0:8, :], regs[cols - 8 : cols, :])
    total = jnp.zeros((8, lats), jnp.float32)
    for k in range(tags):
        ends = jnp.concatenate([acc[k, H : 2 * H], acc[k, cols : cols + H]], axis=0)
        total += jnp.where(here == tag0 + k, turned(ends)[0], 0.0)
    part2[...] = total
    late = spread(part2, got2, g2s, g2r)

    @pl.loop(0, tags)
    def _(k):
        for i in (0, cols // 8 - 1):
            lam_ref[k, :, 8 * i : 8 * i + 8, :] = turned(state[k, H + 8 * i : H + 8 * i + 8])

    for c in early:
        c.wait_recv()
    grad_ref[...] = lax.fori_loop(
        0, groups - 1, lambda d, v: v + got1[d], part1[...]
    )
    for c in late:
        c.wait_recv()
    ends = lax.fori_loop(0, groups - 1, lambda d, v: v + got2[d], part2[...])
    grad_ref[0:8, :] += jnp.where(row < H, ends, 0.0)
    grad_ref[cols - 8 : cols, :] += jnp.where(row >= H, ends, 0.0)

    for c in sends + xsends + [share] + early + late:
        c.wait_send()


def local(
    adjoint_state, east_wind, north_wind, east_diff, north_diff, mass_flux, region_map, cloud_top
):
    tags, levels, cols, lats = adjoint_state.shape
    groups = lax.axis_size("grp")
    f32 = jnp.float32
    wide = cols + 2 * ITERS
    dma = pltpu.SemaphoreType.DMA
    scratch = [
        pltpu.VMEM((tags, levels, cols, lats), f32),
        pltpu.VMEM((5, levels, cols, lats), f32),
        pltpu.VMEM((tags, wide, levels, lats), f32),
        pltpu.VMEM((6, wide, levels, lats), f32),
        pltpu.VMEM((cols, lats), jnp.int32),
        pltpu.VMEM((cols, lats), jnp.int32),
        pltpu.VMEM((tags, levels, 2 * ITERS, lats), f32),
        pltpu.VMEM((5, levels, 2 * ITERS, lats), f32),
        pltpu.VMEM((2 * ITERS, lats), jnp.int32),
        pltpu.VMEM((tags, ITERS, levels, lats), f32),
        pltpu.VMEM((tags, ITERS, levels, lats), f32),
        pltpu.VMEM((levels, lats), f32),
        pltpu.VMEM((tags, wide, 8, lats), f32),
        pltpu.VMEM((cols, lats), f32),
        pltpu.VMEM((2 * ITERS, lats), f32),
        pltpu.VMEM((groups - 1, cols, lats), f32),
        pltpu.VMEM((groups - 1, 2 * ITERS, lats), f32),
        dma((8,)),
        dma((2, tags // 2)),
        dma((2, tags // 2)),
        dma((2, 6)),
        dma((2, 6)),
        dma,
        dma,
        dma((groups - 1,)),
        dma((groups - 1,)),
        dma((groups - 1,)),
        dma((groups - 1,)),
    ]
    return pl.pallas_call(
        kernel,
        name="adjoint_transport",
        out_shape=(
            pltpu.VMEM((tags, levels, cols, lats), f32),
            pltpu.VMEM((cols, lats), f32),
        ),
        in_specs=[pl.BlockSpec(memory_space=pltpu.HBM)] * 8,
        out_specs=(
            pl.BlockSpec(memory_space=pltpu.VMEM),
            pl.BlockSpec(memory_space=pltpu.VMEM),
        ),
        scratch_shapes=scratch,
        compiler_params=pltpu.CompilerParams(
            collective_id=0, has_side_effects=True, vmem_limit_bytes=58 << 20
        ),
    )(
        adjoint_state, east_wind, north_wind, east_diff, north_diff, mass_flux, region_map,
        cloud_top,
    )


def solution(mesh):
    return jax.shard_map(
        local,
        mesh=mesh,
        in_specs=(
            P("grp", None, "dom", None),
            P(None, "dom", None),
            P(None, "dom", None),
            P(None, "dom", None),
            P(None, "dom", None),
            P(None, "dom", None),
            P("dom", None),
            P("dom", None),
        ),
        out_specs=(P("grp", None, "dom", None), P("dom", None)),
        check_vma=False,
    )
```

time: 146 us -> 48.7 us (0.33); the launches traced: 144 us -> 48.6 us
  blocking collectives: 53.5 us -> 0 us
  Pallas kernels: 0 us -> 46 us
  starting transfers between devices: 37.7 us -> 0 us
  local copies, waits for them, and re-layouts: 19.3 us -> 1.94 us
  other arithmetic: 16.4 us -> 0 us
  waiting for transfers between devices: 16.1 us -> 0 us
    psum x1 -> x0, blocking collectives: 53.5 us -> none  [local(): flux_gradient = lax.psum(local_grad, 'grp')]
    pallas_call x0 -> x1, Pallas kernels: none -> 46 us  [local(): pl.pallas_call(kernel, name='adjoint_transport', out_shape=(pltpu.VMEM((t...]
    ppermute x9 -> x0, starting transfers between devices: 37.7 us -> none  [the longest x4 22.8 us: with_halo(): lax.ppermute(head, axis, [((i + 1) % count, i) for i in range(count)])]
    ppermute x9 -> x0, waiting for transfers between devices: 16.1 us -> none  [the longest x4 16 us: with_halo(): lax.ppermute(tail, axis, [(i, (i + 1) % count) for i in range(count)])]
    add x9 -> x0, other arithmetic: 10.5 us -> none  [the longest x4 8 us: local(): center + coef_e * (east - center) + coef_w * (west - center)]
    slice x23 -> x0, local copies, waits for them, and re-layouts: 10.4 us -> none  [the longest x8 7.72 us: local(): south = jnp.concatenate([center[..., :1], center[..., :-1]], axis=-1)]
    unnamed x20 -> x2, local copies, waits for them, and re-layouts: 8.83 us -> 1.94 us
    another operation x2 -> x0, other arithmetic: 3.05 us -> none  [local(): stacked = jnp.stack([east_wind, east_diff, north_wind, north_diff, active])]
  transfers between devices with their start and end apart: 9 -> 0, of which waited for: 3 -> 0; matrix products, arithmetic and copies ran while one was open for 12% -> 0% of each run, Pallas kernels for 0% -> 0%
where the time goes in v1:
time: 48.7 us; the launch traced here: 48.6 us
  Pallas kernels  46 us (94%)
  local copies, waits for them, and re-layouts  1.94 us (4%)
  between operations  0.64 us (1%)
    pallas_call x1, Pallas kernels, local(): pl.pallas_call(kernel, name='adjoint_transport', out_shape=(pltpu.VMEM((t...  46 us
    unnamed x2, local copies, waits for them, and re-layouts  1.94 us

profile of v1, /device:TPU:1, one launch (start us, length us, event | category | flops | bytes accessed | tf_op | source)
XLA Modules:
  0.0 48.6 jit_solution(17547652227754722011)
XLA Ops:
  0.6 46.0 %adjoint_transport.1 = (f32[4,16,32,256]{3,2,1,0:T(8,128)S(1)}, f32[32,256]{1,0:T(8,128)S(1)}) custom-call(f32[4,16,32,256]{3,2,1,0:T(8,128)} %x_ref.1, f32[16,32,256]{2,1,0:T(8,128)} %ew_ref.1, f32[16,32,256]{2,1,0:T(8,128)} %nw_ref.1, f32[16,32,256]{2,1,0:T(8,128)} %ed_ref.1, f32[16,32,256]{2,1,0:T(8,128)} %nd_ref.1, f32[16,32,256]{2,1,0:T(8,128)} %mf_ref.1, ...), custom_call_target="tpu_custom_call" | custom-call | tf_op jit(solution)/shard_map/adjoint_transport/pallas_call | solution.py:303
  46.6 1.3 %copy.12 = f32[4,16,32,256]{3,2,1,0:T(8,128)} copy(f32[4,16,32,256]{3,2,1,0:T(8,128)S(1)} %get-tuple-element.2) | data formatting | bytes 4194304
  47.9 0.6 %copy.13 = f32[32,256]{1,0:T(8,128)} copy(f32[32,256]{1,0:T(8,128)S(1)} %get-tuple-element.3) | data formatting | bytes 65536

commit v2 on v1

--- a/solution.py
+++ b/solution.py
@@ -18,8 +18,8 @@
     x_ref, ew_ref, nw_ref, ed_ref, nd_ref, mf_ref, reg_ref, top_ref,
     lam_ref, grad_ref,
     raw, wraw, state, coef, ctop, regs, halo, whalo, thalo, save_l, save_r, west_end,
-    acc, part1, part2, got1, got2,
-    in_sem, xs_sem, xr_sem, ws_sem, wr_sem, fs_sem, fr_sem, g1s, g1r, g2s, g2r,
+    acc, part1, part2, got1, got2, surf, keep_first,
+    in_sem, xs_sem, xr_sem, ws_sem, wr_sem, ts_sem, tr_sem, fs_sem, fr_sem, g1s, g1r, g2s, g2r,
 ):
     tags, levels, cols, lats = x_ref.shape
     groups = lax.axis_size("grp")
@@ -31,7 +31,7 @@
     half = lax.rem(grp, 2)
     twin = grp + 1 - 2 * half
     H = ITERS
-    hl = levels // 2
+    low = ITERS + 2
 
     winds = (ew_ref, ed_ref, nw_ref, nd_ref, mf_ref)
     barrier = pltpu.get_barrier_semaphore()
@@ -48,10 +48,68 @@
     for c in loads:
         c.start()
 
-    lane = lax.broadcasted_iota(jnp.int32, (8, levels, lats), 2)
-    level = lax.broadcasted_iota(jnp.int32, (levels, 8, lats), 0)
+    pl.semaphore_wait(barrier, groups + 1)
+
+    sides = ((0, east_dev, cols - H, 0), (1, west_dev, 0, H))
+    spans = ((0, low // 2), (low, (levels - low) // 2))
+    mine = [pl.ds(lo + half * n, n) for lo, n in spans]
+
+    def wind_sends(part):
+        out = []
+        for s, q, src, dst in sides:
+            for a, w in enumerate(winds):
+                out.append(
+                    pltpu.make_async_remote_copy(
+                        w.at[mine[part], src : src + H, :],
+                        whalo.at[a, mine[part], dst : dst + H, :],
+                        ws_sem.at[part, s, a], wr_sem.at[part, s, a],
+                        device_id={"dom": q}, device_id_type=MESH,
+                    )
+                )
+        for c in out:
+            c.start()
+        return out
+
+    def state_sends(at, tag, lev):
+        out = []
+        for s, q, src, dst in sides:
+            out.append(
+                pltpu.make_async_remote_copy(
+                    x_ref.at[tag, lev, src : src + H, :],
+                    halo.at[tag, lev, dst : dst + H, :],
+                    xs_sem.at[at, s], xr_sem.at[at, s],
+                    device_id={"dom": q}, device_id_type=MESH,
+                )
+            )
+        for c in out:
+            c.start()
+        return out
+
+    low_winds = wind_sends(0)
+    tops = []
+    for s, q, src, dst in sides:
+        c = pltpu.make_async_remote_copy(
+            top_ref.at[src : src + H, :], thalo.at[dst : dst + H, :],
+            ts_sem.at[s], tr_sem.at[s],
+            device_id={"dom": q}, device_id_type=MESH,
+        )
+        c.start()
+        tops.append(c)
+    low_state = state_sends(0, slice(0, tags), slice(0, low))
+    high_winds = wind_sends(1)
+    high_state = [
+        state_sends(1 + p, slice(2 * p, 2 * p + 2), slice(low, levels)) for p in range(tags // 2)
+    ]
+
+    def share_part(part):
+        return pltpu.make_async_remote_copy(
+            whalo.at[:, mine[part]], whalo.at[:, mine[part]], fs_sem.at[part], fr_sem.at[part],
+            device_id={"grp": twin}, device_id_type=MESH,
+        )
 
     def derive(ew, ed, nw, nd, mf, top, before):
+        level = lax.broadcasted_iota(jnp.int32, ew.shape, 0)
+        lane = lax.broadcasted_iota(jnp.int32, (8, ew.shape[0], lats), 2)
         lift = mf * (level < jnp.minimum(top, levels - 1)[None]).astype(jnp.float32)
         ew, ed, nw, nd, lift = turned(ew), turned(ed), turned(nw), turned(nd), turned(lift)
         east = jnp.maximum(ew, 0.0) + ed
@@ -76,6 +134,7 @@
         0, cols // 8, derive_tile, jnp.zeros((levels, lats), jnp.float32)
     )
 
+    keep_first[...] = coef[C0, H]
     loads[7].wait()
     loads[6].wait()
 
@@ -84,54 +143,19 @@
         for i in range(cols // 8):
             state[k, pl.ds(H + 8 * i, 8)] = turned(raw[k, :, 8 * i : 8 * i + 8, :])
 
-    pl.semaphore_wait(barrier, groups + 1)
-
-    mine = pl.ds(pl.multiple_of(half * hl, hl), hl)
-    sends = []
-    sides = ((0, east_dev, cols - H, 0), (1, west_dev, 0, H))
-    for s, q, src, dst in sides:
-        for a, w in enumerate(winds):
-            sends.append(
-                pltpu.make_async_remote_copy(
-                    w.at[mine, src : src + H, :],
-                    whalo.at[a, mine, dst : dst + H, :],
-                    ws_sem.at[s, a], wr_sem.at[s, a],
-                    device_id={"dom": q}, device_id_type=MESH,
-                )
-            )
-        sends.append(
-            pltpu.make_async_remote_copy(
-                top_ref.at[src : src + H, :], thalo.at[dst : dst + H, :],
-                ws_sem.at[s, 5], wr_sem.at[s, 5],
-                device_id={"dom": q}, device_id_type=MESH,
-            )
-        )
-    for c in sends:
-        c.start()
-    xsends = []
-    for p in range(tags // 2):
-        for s, q, src, dst in sides:
-            c = pltpu.make_async_remote_copy(
-                x_ref.at[2 * p : 2 * p + 2, :, src : src + H, :],
-                halo.at[2 * p : 2 * p + 2, :, dst : dst + H, :],
-                xs_sem.at[s, p], xr_sem.at[s, p],
-                device_id={"dom": q}, device_id_type=MESH,
-            )
-            c.start()
-            xsends.append(c)
-
     def advance(left, cen, right, c):
+        lv = pl.ds(0, cen.shape[1])
         north = pltpu.roll(cen, lats - 1, 2)
         south = pltpu.roll(cen, 1, 2)
         h = (
-            coef[C0, c][None] * cen
-            + coef[CE, c][None] * right
-            + coef[CW, c][None] * left
-            + coef[CN, c][None] * north
-            + coef[CS, c][None] * south
+            coef[C0, c, lv][None] * cen
+            + coef[CE, c, lv][None] * right
+            + coef[CW, c, lv][None] * left
+            + coef[CN, c, lv][None] * north
+            + coef[CS, c, lv][None] * south
         )
-        above = pltpu.roll(h, levels - 1, 1)
-        return h + coef[UP, c][None] * (above - h)
+        above = pltpu.roll(h, cen.shape[1] - 1, 1)
+        return h + coef[UP, c, lv][None] * (above - h)
 
     acc[...] = jnp.zeros_like(acc)
 
@@ -139,22 +163,25 @@
     def _(p):
         ks = pl.ds(2 * p, 2)
 
-        @pl.loop(1, ITERS + 1)
-        def _(t):
-            left = state[ks, H + t - 1]
-            cen = state[ks, H + t]
-            save_l[ks, t - 1] = cen
-
-            def body(c, carry):
-                left, cen = carry
-                right = state[ks, c + 1]
-                new = advance(left, cen, right, c)
-                state[ks, c] = new
-                acc[ks, c] += new[:, 0:8]
-                return cen, right
-
-            left, cen = lax.fori_loop(H + t, H + cols - t, body, (left, cen))
-            save_r[ks, t - 1] = left
+        def run(c, carry, n):
+            old = list(carry) + [state[ks, c + 1 + j] for j in range(n)]
+            for j in range(n):
+                new = advance(old[j], old[j + 1], old[j + 2], c + j)
+                state[ks, c + j] = new
+                acc[ks, c + j] += new[:, 0:8]
+            return old[n], old[n + 1]
+
+        for t in range(1, ITERS + 1):
+            start, size = H + t, cols - 2 * t
+            carry = state[ks, start - 1], state[ks, start]
+            save_l[ks, t - 1] = carry[1]
+            if size % 4:
+                carry = run(start, carry, size % 4)
+                start += size % 4
+            carry = lax.fori_loop(
+                0, size // 4, lambda b, v: run(start + 4 * b, v, 4), carry
+            )
+            save_r[ks, t - 1] = carry[0]
 
     tag0 = grp * tags
     row = lax.broadcasted_iota(jnp.int32, (8, lats), 0)
@@ -187,52 +214,68 @@
         for i in range(1, cols // 8 - 1):
             lam_ref[k, :, 8 * i : 8 * i + 8, :] = turned(state[k, H + 8 * i : H + 8 * i + 8])
 
-    for c in sends:
-        c.wait_recv()
-    share = pltpu.make_async_remote_copy(
-        whalo.at[:, mine], whalo.at[:, mine], fs_sem, fr_sem,
-        device_id={"grp": twin}, device_id_type=MESH,
-    )
-    share.start()
-    share.wait_recv()
-
-    made, prime = derive(*[whalo[a] for a in range(5)], thalo[...], jnp.zeros((levels, lats), jnp.float32))
-    for m in range(6):
-        coef[m, 0:H] = made[m][0:H]
-        coef[m, H + cols : 2 * H + cols] = made[m][H:]
-    first = prime[H - 1]
-    coef[CW, H] = first
-    coef[C0, H] = coef[C0, H] - first
-    last = west_end[...]
-    coef[CW, H + cols] = last
-    coef[C0, H + cols] = made[C0][H] + made[CW][H] - last
-
-    for p in range(tags // 2):
-        for c in xsends[2 * p : 2 * p + 2]:
-            c.wait_recv()
-        for k in (2 * p, 2 * p + 1):
-            edge = turned(halo[k])
-            state[k, 0:H] = edge[0:H]
-            state[k, H + cols : 2 * H + cols] = edge[H:]
-        ks = pl.ds(2 * p, 2)
-
+    def edge_coefs(lv, size):
+        pad = levels // 2 * (size < levels)
+
+        def part(a):
+            if not pad:
+                return whalo[a]
+            return jnp.concatenate(
+                [whalo[a, 0:size], jnp.zeros((pad - size, 2 * H, lats), jnp.float32)], axis=0
+            )
+
+        made, prime = derive(
+            *[part(a) for a in range(5)], thalo[...], jnp.zeros((lv.size, lats), jnp.float32)
+        )
+        for m in range(6):
+            coef[m, 0:H, lv] = made[m][0:H]
+            coef[m, H + cols : 2 * H + cols, lv] = made[m][H:]
+        first = prime[H - 1]
+        coef[CW, H, lv] = first
+        coef[C0, H, lv] = keep_first[lv] - first
+        last = west_end[lv]
+        coef[CW, H + cols, lv] = last
+        coef[C0, H + cols, lv] = made[C0][H] + made[CW][H] - last
+
+    def edges(store, ks, lv, shift, count_in):
         @pl.loop(1, ITERS + 1)
         def _(t):
-            left, cen = state[ks, t - 1], state[ks, t]
-            for n in range(H):
-                right = state[ks, t + n + 1] if n < H - 1 else save_l[ks, t - 1]
-                new = advance(left, cen, right, t + n)
-                state[ks, t + n] = new
-                acc[ks, t + n] += new[:, 0:8]
-                left, cen = cen, right
-            base = H + cols - t
-            left, cen = save_r[ks, t - 1], state[ks, base]
-            for n in range(H):
-                right = state[ks, base + n + 1]
-                new = advance(left, cen, right, base + n)
-                state[ks, base + n] = new
-                acc[ks, base + n] += new[:, 0:8]
-                left, cen = cen, right
+            for base, at in ((t, t), (H + cols - t, H + cols - t - shift)):
+                if base is t:
+                    old = [store[ks, at - 1 + n] for n in range(H + 1)]
+                    old.append(save_l[ks, t - 1, lv])
+                else:
+                    old = [save_r[ks, t - 1, lv]]
+                    old += [store[ks, at + n] for n in range(H + 1)]
+                for n in range(H):
+                    new = advance(old[n], old[n + 1], old[n + 2], base + n)
+                    store[ks, at + n] = new
+                    if count_in:
+                        acc[ks, base + n] += new
+
+    for c in low_winds:
+        c.wait_recv()
+    share0 = share_part(0)
+    share0.start()
+    for c in tops + low_state:
+        c.wait_recv()
+    share0.wait_recv()
+    edge_coefs(pl.ds(0, 8), low)
+
+    @pl.loop(0, tags // 2)
+    def _(p):
+        for j in range(2):
+            k = 2 * p + j
+            ring = turned(
+                jnp.concatenate(
+                    [halo[k, 0:low], jnp.zeros((8 - low, 2 * H, lats), jnp.float32)], axis=0
+                )
+            )
+            surf[k, 0:H] = ring[0:H]
+            surf[k, 3 * H : 4 * H] = ring[H:]
+            surf[k, H : 2 * H] = state[k, H : 2 * H, 0:8]
+            surf[k, 2 * H : 3 * H] = state[k, cols : cols + H, 0:8]
+        edges(surf, pl.ds(2 * p, 2), pl.ds(0, 8), cols - 2 * H, True)
 
     here = jnp.where(row < H, regs[0:8, :], regs[cols - 8 : cols, :])
     total = jnp.zeros((8, lats), jnp.float32)
@@ -242,10 +285,24 @@
     part2[...] = total
     late = spread(part2, got2, g2s, g2r)
 
-    @pl.loop(0, tags)
-    def _(k):
-        for i in (0, cols // 8 - 1):
-            lam_ref[k, :, 8 * i : 8 * i + 8, :] = turned(state[k, H + 8 * i : H + 8 * i + 8])
+    for c in high_winds:
+        c.wait_recv()
+    share1 = share_part(1)
+    share1.start()
+    share1.wait_recv()
+    edge_coefs(pl.ds(0, levels), levels)
+
+    for p in range(tags // 2):
+        for c in high_state[p]:
+            c.wait_recv()
+        for k in (2 * p, 2 * p + 1):
+            ring = turned(halo[k])
+            state[k, 0:H] = ring[0:H]
+            state[k, H + cols : 2 * H + cols] = ring[H:]
+        edges(state, pl.ds(2 * p, 2), pl.ds(0, levels), 0, False)
+        for k in (2 * p, 2 * p + 1):
+            for i in (0, cols // 8 - 1):
+                lam_ref[k, :, 8 * i : 8 * i + 8, :] = turned(state[k, H + 8 * i : H + 8 * i + 8])
 
     for c in early:
         c.wait_recv()
@@ -258,7 +315,8 @@
     grad_ref[0:8, :] += jnp.where(row < H, ends, 0.0)
     grad_ref[cols - 8 : cols, :] += jnp.where(row >= H, ends, 0.0)
 
-    for c in sends + xsends + [share] + early + late:
+    sent = low_winds + tops + low_state + high_winds + high_state[0] + high_state[1]
+    for c in sent + [share0, share1] + early + late:
         c.wait_send()
 
 
@@ -288,13 +346,17 @@
         pltpu.VMEM((2 * ITERS, lats), f32),
         pltpu.VMEM((groups - 1, cols, lats), f32),
         pltpu.VMEM((groups - 1, 2 * ITERS, lats), f32),
+        pltpu.VMEM((tags, 4 * ITERS, 8, lats), f32),
+        pltpu.VMEM((levels, lats), f32),
         dma((8,)),
-        dma((2, tags // 2)),
-        dma((2, tags // 2)),
-        dma((2, 6)),
-        dma((2, 6)),
-        dma,
-        dma,
+        dma((1 + tags // 2, 2)),
+        dma((1 + tags // 2, 2)),
+        dma((2, 2, 5)),
+        dma((2, 2, 5)),
+        dma((2,)),
+        dma((2,)),
+        dma((2,)),
+        dma((2,)),
         dma((groups - 1,)),
         dma((groups - 1,)),
         dma((groups - 1,)),

time: 48.7 us -> 38.1 us (0.78)
  Pallas kernels: 46 us -> 35.4 us
    pallas_call x1, Pallas kernels: 46 us -> 35.4 us  [local(): pl.pallas_call(kernel, name='adjoint_transport', out_shape=(pltpu.VMEM((t...]
where the time goes in v2:
time: 38.1 us; the launch traced here: 38 us
  Pallas kernels  35.4 us (93%)
  local copies, waits for them, and re-layouts  1.94 us (5%)
  between operations  0.64 us (2%)
    pallas_call x1, Pallas kernels, local(): pl.pallas_call(kernel, name='adjoint_transport', out_shape=(pltpu.VMEM((t...  35.4 us
    unnamed x2, local copies, waits for them, and re-layouts  1.94 us

profile of v2, /device:TPU:1, one launch (start us, length us, event | category | flops | bytes accessed | tf_op | source)
XLA Modules:
  0.0 38.0 jit_solution(4539151847265839048)
XLA Ops:
  0.6 35.4 %adjoint_transport.1 = (f32[4,16,32,256]{3,2,1,0:T(8,128)S(1)}, f32[32,256]{1,0:T(8,128)S(1)}) custom-call(f32[4,16,32,256]{3,2,1,0:T(8,128)} %x_ref.1, f32[16,32,256]{2,1,0:T(8,128)} %ew_ref.1, f32[16,32,256]{2,1,0:T(8,128)} %nw_ref.1, f32[16,32,256]{2,1,0:T(8,128)} %ed_ref.1, f32[16,32,256]{2,1,0:T(8,128)} %nd_ref.1, f32[16,32,256]{2,1,0:T(8,128)} %mf_ref.1, ...), custom_call_target="tpu_custom_call" | custom-call | tf_op jit(solution)/shard_map/adjoint_transport/pallas_call | solution.py:365
  36.0 1.3 %copy.12 = f32[4,16,32,256]{3,2,1,0:T(8,128)} copy(f32[4,16,32,256]{3,2,1,0:T(8,128)S(1)} %get-tuple-element.2) | data formatting | bytes 4194304
  37.4 0.6 %copy.13 = f32[32,256]{1,0:T(8,128)} copy(f32[32,256]{1,0:T(8,128)S(1)} %get-tuple-element.3) | data formatting | bytes 65536

commit v3 on v2

--- a/solution.py
+++ b/solution.py
@@ -18,8 +18,8 @@
     x_ref, ew_ref, nw_ref, ed_ref, nd_ref, mf_ref, reg_ref, top_ref,
     lam_ref, grad_ref,
     raw, wraw, state, coef, ctop, regs, halo, whalo, thalo, save_l, save_r, west_end,
-    acc, part1, part2, got1, got2, surf, keep_first,
-    in_sem, xs_sem, xr_sem, ws_sem, wr_sem, ts_sem, tr_sem, fs_sem, fr_sem, g1s, g1r, g2s, g2r,
+    acc, edge_acc, part1, part2, near1, near2, mid1, mid2, far1, far2, surf, keep_first,
+    in_sem, xs_sem, xr_sem, ws_sem, wr_sem, ts_sem, tr_sem, fs_sem, fr_sem, n1_sem, n2_sem, f1_sem, f2_sem,
 ):
     tags, levels, cols, lats = x_ref.shape
     groups = lax.axis_size("grp")
@@ -30,6 +30,9 @@
     west_dev = lax.rem(me + count - 1, count)
     half = lax.rem(grp, 2)
     twin = grp + 1 - 2 * half
+    lane4 = lax.rem(grp, 4)
+    near = [grp - lane4 + lax.rem(lane4 + d, 4) for d in range(1, 4)]
+    far = [lax.rem(grp + 4 * d, groups) for d in range(1, groups // 4)]
     H = ITERS
     low = ITERS + 2
 
@@ -37,10 +40,8 @@
     barrier = pltpu.get_barrier_semaphore()
     for q in (east_dev, west_dev):
         pl.semaphore_signal(barrier, inc=1, device_id={"dom": q}, device_id_type=MESH)
-    for d in range(1, groups):
-        pl.semaphore_signal(
-            barrier, inc=1, device_id={"grp": lax.rem(grp + d, groups)}, device_id_type=MESH
-        )
+    for q in near + far:
+        pl.semaphore_signal(barrier, inc=1, device_id={"grp": q}, device_id_type=MESH)
     loads = [pltpu.make_async_copy(w, wraw.at[a], in_sem.at[a]) for a, w in enumerate(winds)]
     loads.append(pltpu.make_async_copy(top_ref, ctop, in_sem.at[5]))
     loads.append(pltpu.make_async_copy(reg_ref, regs, in_sem.at[6]))
@@ -48,7 +49,45 @@
     for c in loads:
         c.start()
 
-    pl.semaphore_wait(barrier, groups + 1)
+    def derive(ew, ed, nw, nd, mf, top, before):
+        level = lax.broadcasted_iota(jnp.int32, ew.shape, 0)
+        lane = lax.broadcasted_iota(jnp.int32, (8, ew.shape[0], lats), 2)
+        lift = mf * (level < jnp.minimum(top, levels - 1)[None]).astype(jnp.float32)
+        ew, ed, nw, nd, lift = turned(ew), turned(ed), turned(nw), turned(nd), turned(lift)
+        east = jnp.maximum(ew, 0.0) + ed
+        prime = jnp.maximum(-ew, 0.0) + ed
+        west = jnp.concatenate([before[None], prime[:-1]], axis=0)
+        north = jnp.where(lane < lats - 1, jnp.maximum(nw, 0.0) + nd, 0.0)
+        south = jnp.where(lane > 0, pltpu.roll(jnp.maximum(-nw, 0.0) + nd, 1, 2), 0.0)
+        keep = 1.0 - east - west - north - south
+        return (east, west, north, south, keep, lift), prime
+
+    for c in loads[:6]:
+        c.wait()
+
+    def derive_tile(i, before):
+        at = pl.ds(pl.multiple_of(8 * i, 8), 8)
+        made, prime = derive(*[wraw[a, :, at, :] for a in range(5)], ctop[at, :], before)
+        for m in range(6):
+            coef[m, pl.ds(H + 8 * i, 8)] = made[m]
+        return prime[7]
+
+    west_end[...] = lax.fori_loop(
+        0, cols // 8, derive_tile, jnp.zeros((levels, lats), jnp.float32)
+    )
+
+    keep_first[...] = coef[C0, H]
+    loads[7].wait()
+    loads[6].wait()
+
+    @pl.loop(0, tags)
+    def _(k):
+        @pl.loop(0, cols // 8)
+        def _(i):
+            at = pl.multiple_of(8 * i, 8)
+            state[k, pl.ds(H + 8 * i, 8)] = turned(raw[k, :, pl.ds(at, 8), :])
+
+    pl.semaphore_wait(barrier, 2 + len(near) + len(far))
 
     sides = ((0, east_dev, cols - H, 0), (1, west_dev, 0, H))
     spans = ((0, low // 2), (low, (levels - low) // 2))
@@ -58,10 +97,12 @@
         out = []
         for s, q, src, dst in sides:
             for a, w in enumerate(winds):
+                skip = 1 if s == 0 and a > 1 else 0
+                size = H if s == 0 and a < 2 else H - 1
                 out.append(
                     pltpu.make_async_remote_copy(
-                        w.at[mine[part], src : src + H, :],
-                        whalo.at[a, mine[part], dst : dst + H, :],
+                        w.at[mine[part], src + skip : src + skip + size, :],
+                        whalo.at[a, mine[part], dst + skip : dst + skip + size, :],
                         ws_sem.at[part, s, a], wr_sem.at[part, s, a],
                         device_id={"dom": q}, device_id_type=MESH,
                     )
@@ -107,42 +148,6 @@
             device_id={"grp": twin}, device_id_type=MESH,
         )
 
-    def derive(ew, ed, nw, nd, mf, top, before):
-        level = lax.broadcasted_iota(jnp.int32, ew.shape, 0)
-        lane = lax.broadcasted_iota(jnp.int32, (8, ew.shape[0], lats), 2)
-        lift = mf * (level < jnp.minimum(top, levels - 1)[None]).astype(jnp.float32)
-        ew, ed, nw, nd, lift = turned(ew), turned(ed), turned(nw), turned(nd), turned(lift)
-        east = jnp.maximum(ew, 0.0) + ed
-        prime = jnp.maximum(-ew, 0.0) + ed
-        west = jnp.concatenate([before[None], prime[:-1]], axis=0)
-        north = jnp.where(lane < lats - 1, jnp.maximum(nw, 0.0) + nd, 0.0)
-        south = jnp.where(lane > 0, pltpu.roll(jnp.maximum(-nw, 0.0) + nd, 1, 2), 0.0)
-        keep = 1.0 - east - west - north - south
-        return (east, west, north, south, keep, lift), prime
-
-    for c in loads[:6]:
-        c.wait()
-
-    def derive_tile(i, before):
-        at = pl.ds(pl.multiple_of(8 * i, 8), 8)
-        made, prime = derive(*[wraw[a, :, at, :] for a in range(5)], ctop[at, :], before)
-        for m in range(6):
-            coef[m, pl.ds(H + 8 * i, 8)] = made[m]
-        return prime[7]
-
-    west_end[...] = lax.fori_loop(
-        0, cols // 8, derive_tile, jnp.zeros((levels, lats), jnp.float32)
-    )
-
-    keep_first[...] = coef[C0, H]
-    loads[7].wait()
-    loads[6].wait()
-
-    @pl.loop(0, tags)
-    def _(k):
-        for i in range(cols // 8):
-            state[k, pl.ds(H + 8 * i, 8)] = turned(raw[k, :, 8 * i : 8 * i + 8, :])
-
     def advance(left, cen, right, c):
         lv = pl.ds(0, cen.shape[1])
         north = pltpu.roll(cen, lats - 1, 2)
@@ -157,18 +162,26 @@
         above = pltpu.roll(h, cen.shape[1] - 1, 1)
         return h + coef[UP, c, lv][None] * (above - h)
 
-    acc[...] = jnp.zeros_like(acc)
+    blank = jnp.zeros((tags, 8, lats), jnp.float32)
+    for c in (H, H + cols - 1):
+        acc[:, c] = blank
+    for n in range(4 * H):
+        edge_acc[:, n] = blank
+
 
     @pl.loop(0, tags // 2)
     def _(p):
         ks = pl.ds(2 * p, 2)
 
-        def run(c, carry, n):
+        def run(c, carry, n, first):
             old = list(carry) + [state[ks, c + 1 + j] for j in range(n)]
             for j in range(n):
                 new = advance(old[j], old[j + 1], old[j + 2], c + j)
                 state[ks, c + j] = new
-                acc[ks, c + j] += new[:, 0:8]
+                if first:
+                    acc[ks, c + j] = new[:, 0:8]
+                else:
+                    acc[ks, c + j] += new[:, 0:8]
             return old[n], old[n + 1]
 
         for t in range(1, ITERS + 1):
@@ -176,43 +189,49 @@
             carry = state[ks, start - 1], state[ks, start]
             save_l[ks, t - 1] = carry[1]
             if size % 4:
-                carry = run(start, carry, size % 4)
+                carry = run(start, carry, size % 4, t == 1)
                 start += size % 4
             carry = lax.fori_loop(
-                0, size // 4, lambda b, v: run(start + 4 * b, v, 4), carry
+                0, size // 4, lambda b, v: run(start + 4 * b, v, 4, t == 1), carry
             )
             save_r[ks, t - 1] = carry[0]
 
     tag0 = grp * tags
     row = lax.broadcasted_iota(jnp.int32, (8, lats), 0)
 
-    for i in range(cols // 8):
-        here = regs[8 * i : 8 * i + 8, :]
+    def chosen(here, lump):
         total = jnp.zeros((8, lats), jnp.float32)
         for k in range(tags):
-            top = turned(acc[k, H + 8 * i : H + 8 * i + 8])[0]
-            total += jnp.where(here == tag0 + k, top, 0.0)
-        part1[8 * i : 8 * i + 8, :] = total
-
-    def spread(part, got, ss, rs):
+            total += jnp.where(here == tag0 + k, turned(lump[k])[0], 0.0)
+        return total
+
+    @pl.loop(0, cols // 8)
+    def _(i):
+        here = regs[pl.ds(pl.multiple_of(8 * i, 8), 8), :]
+        part1[pl.ds(pl.multiple_of(8 * i, 8), 8), :] = chosen(
+            here, [acc[k, pl.ds(H + 8 * i, 8)] for k in range(tags)]
+        )
+
+    def to_peers(part, got, sems, peers):
         out = []
-        for d in range(1, groups):
+        for n, q in enumerate(peers):
             c = pltpu.make_async_remote_copy(
-                part, got.at[d - 1], ss.at[d - 1], rs.at[d - 1],
-                device_id={"grp": lax.rem(grp + d, groups)}, device_id_type=MESH,
+                part, got.at[n], sems.at[0, n], sems.at[1, n],
+                device_id={"grp": q}, device_id_type=MESH,
             )
             c.start()
             out.append(c)
         return out
 
-    early = spread(part1, got1, g1s, g1r)
-
-    @pl.loop(0, tags)
-    def _(k):
-        for s in (0, H + cols - 4):
-            acc[k, s : s + 8] = jnp.zeros((8, 8, lats), jnp.float32)
-        for i in range(1, cols // 8 - 1):
-            lam_ref[k, :, 8 * i : 8 * i + 8, :] = turned(state[k, H + 8 * i : H + 8 * i + 8])
+    def gathered(part, got, copies):
+        for c in copies:
+            c.wait_recv()
+        value = part[...]
+        for n in range(len(copies)):
+            value += got[n]
+        return value
+
+    early_near = to_peers(part1, near1, n1_sem, near)
 
     def edge_coefs(lv, size):
         pad = levels // 2 * (size < levels)
@@ -251,7 +270,7 @@
                     new = advance(old[n], old[n + 1], old[n + 2], base + n)
                     store[ks, at + n] = new
                     if count_in:
-                        acc[ks, base + n] += new
+                        edge_acc[ks, at + n] += new
 
     for c in low_winds:
         c.wait_recv()
@@ -278,17 +297,25 @@
         edges(surf, pl.ds(2 * p, 2), pl.ds(0, 8), cols - 2 * H, True)
 
     here = jnp.where(row < H, regs[0:8, :], regs[cols - 8 : cols, :])
-    total = jnp.zeros((8, lats), jnp.float32)
-    for k in range(tags):
-        ends = jnp.concatenate([acc[k, H : 2 * H], acc[k, cols : cols + H]], axis=0)
-        total += jnp.where(here == tag0 + k, turned(ends)[0], 0.0)
-    part2[...] = total
-    late = spread(part2, got2, g2s, g2r)
-
+    part2[...] = chosen(here, [edge_acc[k, H : 3 * H] for k in range(tags)])
+
+    late_near = to_peers(part2, near2, n2_sem, near)
+
+    @pl.loop(0, tags)
+    def _(k):
+        @pl.loop(1, cols // 8 - 1)
+        def _(i):
+            at = pl.ds(pl.multiple_of(8 * i, 8), 8)
+            lam_ref[k, :, at, :] = turned(state[k, pl.ds(H + 8 * i, 8)])
+
+    mid1[...] = gathered(part1, near1, early_near)
+    early_far = to_peers(mid1, far1, f1_sem, far)
     for c in high_winds:
         c.wait_recv()
     share1 = share_part(1)
     share1.start()
+    mid2[...] = gathered(part2, near2, late_near)
+    late_far = to_peers(mid2, far2, f2_sem, far)
     share1.wait_recv()
     edge_coefs(pl.ds(0, levels), levels)
 
@@ -304,20 +331,25 @@
             for i in (0, cols // 8 - 1):
                 lam_ref[k, :, 8 * i : 8 * i + 8, :] = turned(state[k, H + 8 * i : H + 8 * i + 8])
 
-    for c in early:
-        c.wait_recv()
-    grad_ref[...] = lax.fori_loop(
-        0, groups - 1, lambda d, v: v + got1[d], part1[...]
-    )
-    for c in late:
-        c.wait_recv()
-    ends = lax.fori_loop(0, groups - 1, lambda d, v: v + got2[d], part2[...])
+    grad_ref[...] = gathered(mid1, far1, early_far)
+    ends = gathered(mid2, far2, late_far)
     grad_ref[0:8, :] += jnp.where(row < H, ends, 0.0)
     grad_ref[cols - 8 : cols, :] += jnp.where(row >= H, ends, 0.0)
 
     sent = low_winds + tops + low_state + high_winds + high_state[0] + high_state[1]
-    for c in sent + [share0, share1] + early + late:
+    for c in sent + [share0, share1] + early_near + early_far + late_near + late_far:
         c.wait_send()
+
+
+def write_out(lam_ref, grad_ref, lam_out, grad_out, sem):
+    copies = [
+        pltpu.make_async_copy(lam_ref, lam_out, sem.at[0]),
+        pltpu.make_async_copy(grad_ref, grad_out, sem.at[1]),
+    ]
+    for c in copies:
+        c.start()
+    for c in copies:
+        c.wait()
 
 
 def local(
@@ -342,10 +374,15 @@
         pltpu.VMEM((tags, ITERS, levels, lats), f32),
         pltpu.VMEM((levels, lats), f32),
         pltpu.VMEM((tags, wide, 8, lats), f32),
+        pltpu.VMEM((tags, 4 * ITERS, 8, lats), f32),
         pltpu.VMEM((cols, lats), f32),
         pltpu.VMEM((2 * ITERS, lats), f32),
-        pltpu.VMEM((groups - 1, cols, lats), f32),
-        pltpu.VMEM((groups - 1, 2 * ITERS, lats), f32),
+        pltpu.VMEM((3, cols, lats), f32),
+        pltpu.VMEM((3, 2 * ITERS, lats), f32),
+        pltpu.VMEM((cols, lats), f32),
+        pltpu.VMEM((2 * ITERS, lats), f32),
+        pltpu.VMEM((groups // 4 - 1, cols, lats), f32),
+        pltpu.VMEM((groups // 4 - 1, 2 * ITERS, lats), f32),
         pltpu.VMEM((tags, 4 * ITERS, 8, lats), f32),
         pltpu.VMEM((levels, lats), f32),
         dma((8,)),
@@ -357,12 +394,12 @@
         dma((2,)),
         dma((2,)),
         dma((2,)),
-        dma((groups - 1,)),
-        dma((groups - 1,)),
-        dma((groups - 1,)),
-        dma((groups - 1,)),
+        dma((2, 3)),
+        dma((2, 3)),
+        dma((2, groups // 4 - 1)),
+        dma((2, groups // 4 - 1)),
     ]
-    return pl.pallas_call(
+    made = pl.pallas_call(
         kernel,
         name="adjoint_transport",
         out_shape=(
@@ -382,6 +419,14 @@
         adjoint_state, east_wind, north_wind, east_diff, north_diff, mass_flux, region_map,
         cloud_top,
     )
+    return pl.pallas_call(
+        write_out,
+        name="write_out",
+        out_shape=tuple(jax.ShapeDtypeStruct(v.shape, v.dtype) for v in made),
+        in_specs=[pl.BlockSpec(memory_space=pltpu.VMEM)] * 2,
+        out_specs=(pl.BlockSpec(memory_space=pltpu.HBM),) * 2,
+        scratch_shapes=[dma((2,))],
+    )(*[pltpu.with_memory_space_constraint(v, pltpu.VMEM) for v in made])
 
 
 def solution(mesh):

time: 38.1 us -> 35.2 us (0.924)
  local copies, waits for them, and re-layouts: 1.94 us -> 0 us
  Pallas kernels: 35.4 us -> 34.4 us
    pallas_call x1, Pallas kernels: 35.4 us -> 33.1 us  [local(): pl.pallas_call(kernel, name='adjoint_transport', out_shape=(pltpu.VMEM((t...]
    unnamed x2 -> x0, local copies, waits for them, and re-layouts: 1.94 us -> none
    pallas_call x0 -> x1, Pallas kernels: none -> 1.34 us  [local(): pl.pallas_call(write_out, name='write_out', out_shape=tuple((jax.ShapeDty...]
where the time goes in v3:
time: 35.2 us; the launch traced here: 35.1 us
  Pallas kernels  34.4 us (98%)
  between operations  0.64 us (2%)
    pallas_call x1, Pallas kernels, local(): pl.pallas_call(kernel, name='adjoint_transport', out_shape=(pltpu.VMEM((t...  33.1 us
    pallas_call x1, Pallas kernels, local(): pl.pallas_call(write_out, name='write_out', out_shape=tuple((jax.ShapeDty...  1.34 us

profile of v3, /device:TPU:1, one launch (start us, length us, event | category | flops | bytes accessed | tf_op | source)
XLA Modules:
  0.0 35.1 jit_solution(9880617254738041050)
XLA Ops:
  0.6 33.1 %adjoint_transport.1 = (f32[4,16,32,256]{3,2,1,0:T(8,128)S(1)}, f32[32,256]{1,0:T(8,128)S(1)}) custom-call(f32[4,16,32,256]{3,2,1,0:T(8,128)} %x_ref.1, f32[16,32,256]{2,1,0:T(8,128)} %ew_ref.1, f32[16,32,256]{2,1,0:T(8,128)} %nw_ref.1, f32[16,32,256]{2,1,0:T(8,128)} %ed_ref.1, f32[16,32,256]{2,1,0:T(8,128)} %nd_ref.1, f32[16,32,256]{2,1,0:T(8,128)} %mf_ref.1, ...), custom_call_target="tpu_custom_call" | custom-call | tf_op jit(solution)/shard_map/adjoint_transport/pallas_call | solution.py:402
  33.7 1.3 %write_out.1 = (f32[4,16,32,256]{3,2,1,0:T(8,128)}, f32[32,256]{1,0:T(8,128)}) custom-call(f32[4,16,32,256]{3,2,1,0:T(8,128)S(1)} %get-tuple-element.4.lam_ref, f32[32,256]{1,0:T(8,128)S(1)} %get-tuple-element.5.grad_ref), custom_call_target="tpu_custom_call" | custom-call | tf_op jit(solution)/shard_map/write_out/pallas_call | solution.py:422

commit v4 on v3

--- a/solution.py
+++ b/solution.py
@@ -188,11 +188,11 @@
             start, size = H + t, cols - 2 * t
             carry = state[ks, start - 1], state[ks, start]
             save_l[ks, t - 1] = carry[1]
-            if size % 4:
-                carry = run(start, carry, size % 4, t == 1)
-                start += size % 4
+            if size % 8:
+                carry = run(start, carry, size % 8, t == 1)
+                start += size % 8
             carry = lax.fori_loop(
-                0, size // 4, lambda b, v: run(start + 4 * b, v, 4, t == 1), carry
+                0, size // 8, lambda b, v: run(start + 8 * b, v, 8, t == 1), carry
             )
             save_r[ks, t - 1] = carry[0]
 
@@ -308,14 +308,14 @@
             at = pl.ds(pl.multiple_of(8 * i, 8), 8)
             lam_ref[k, :, at, :] = turned(state[k, pl.ds(H + 8 * i, 8)])
 
-    mid1[...] = gathered(part1, near1, early_near)
-    early_far = to_peers(mid1, far1, f1_sem, far)
     for c in high_winds:
         c.wait_recv()
     share1 = share_part(1)
     share1.start()
     mid2[...] = gathered(part2, near2, late_near)
     late_far = to_peers(mid2, far2, f2_sem, far)
+    mid1[...] = gathered(part1, near1, early_near)
+    early_far = to_peers(mid1, far1, f1_sem, far)
     share1.wait_recv()
     edge_coefs(pl.ds(0, levels), levels)
 

time: 35.2 us -> 34.7 us (0.986)
  Pallas kernels: 34.4 us -> 34 us
    pallas_call x1, Pallas kernels: 33.1 us -> 32.6 us  [local(): pl.pallas_call(kernel, name='adjoint_transport', out_shape=(pltpu.VMEM((t...]
where the time goes in v4:
time: 34.7 us; the launch traced here: 34.6 us
  Pallas kernels  34 us (98%)
  between operations  0.64 us (2%)
    pallas_call x1, Pallas kernels, local(): pl.pallas_call(kernel, name='adjoint_transport', out_shape=(pltpu.VMEM((t...  32.6 us
    pallas_call x1, Pallas kernels, local(): pl.pallas_call(write_out, name='write_out', out_shape=tuple((jax.ShapeDty...  1.34 us

profile of v4, /device:TPU:1, one launch (start us, length us, event | category | flops | bytes accessed | tf_op | source)
XLA Modules:
  0.0 34.6 jit_solution(13088577723331415283)
XLA Ops:
  0.6 32.6 %adjoint_transport.1 = (f32[4,16,32,256]{3,2,1,0:T(8,128)S(1)}, f32[32,256]{1,0:T(8,128)S(1)}) custom-call(f32[4,16,32,256]{3,2,1,0:T(8,128)} %x_ref.1, f32[16,32,256]{2,1,0:T(8,128)} %ew_ref.1, f32[16,32,256]{2,1,0:T(8,128)} %nw_ref.1, f32[16,32,256]{2,1,0:T(8,128)} %ed_ref.1, f32[16,32,256]{2,1,0:T(8,128)} %nd_ref.1, f32[16,32,256]{2,1,0:T(8,128)} %mf_ref.1, ...), custom_call_target="tpu_custom_call" | custom-call | tf_op jit(solution)/shard_map/adjoint_transport/pallas_call | solution.py:402
  33.3 1.3 %write_out.1 = (f32[4,16,32,256]{3,2,1,0:T(8,128)}, f32[32,256]{1,0:T(8,128)}) custom-call(f32[4,16,32,256]{3,2,1,0:T(8,128)S(1)} %get-tuple-element.4.lam_ref, f32[32,256]{1,0:T(8,128)S(1)} %get-tuple-element.5.grad_ref), custom_call_target="tpu_custom_call" | custom-call | tf_op jit(solution)/shard_map/write_out/pallas_call | solution.py:422

commit v5 on v4

--- a/solution.py
+++ b/solution.py
@@ -87,6 +87,59 @@
             at = pl.multiple_of(8 * i, 8)
             state[k, pl.ds(H + 8 * i, 8)] = turned(raw[k, :, pl.ds(at, 8), :])
 
+    def advance(left, cen, right, c):
+        lv = pl.ds(0, cen.shape[1])
+        north = pltpu.roll(cen, lats - 1, 2)
+        south = pltpu.roll(cen, 1, 2)
+        h = (
+            coef[C0, c, lv][None] * cen
+            + coef[CE, c, lv][None] * right
+            + coef[CW, c, lv][None] * left
+            + coef[CN, c, lv][None] * north
+            + coef[CS, c, lv][None] * south
+        )
+        above = pltpu.roll(h, cen.shape[1] - 1, 1)
+        return h + coef[UP, c, lv][None] * (above - h)
+
+    blank = jnp.zeros((tags, 8, lats), jnp.float32)
+    for c in (H, H + cols - 1):
+        acc[:, c] = blank
+    for n in range(4 * H):
+        edge_acc[:, n] = blank
+
+
+    def interior(p):
+        ks = pl.ds(2 * p, 2)
+
+        def run(c, carry, n, first):
+            old = list(carry) + [state[ks, c + 1 + j] for j in range(n)]
+            for j in range(n):
+                new = advance(old[j], old[j + 1], old[j + 2], c + j)
+                state[ks, c + j] = new
+                if first:
+                    acc[ks, c + j] = new[:, 0:8]
+                else:
+                    acc[ks, c + j] += new[:, 0:8]
+            return old[n], old[n + 1]
+
+        for t in range(1, ITERS + 1):
+            start, size = H + t, cols - 2 * t
+            carry = state[ks, start - 1], state[ks, start]
+            save_l[ks, t - 1] = carry[1]
+            if size % 8:
+                carry = run(start, carry, size % 8, t == 1)
+                start += size % 8
+            carry = lax.fori_loop(
+                0, size // 8, lambda b, v: run(start + 8 * b, v, 8, t == 1), carry
+            )
+            save_r[ks, t - 1] = carry[0]
+
+    ahead = jnp.where(lax.rem(me, count // 2) < 2, tags // 2, 0)
+
+    @pl.loop(0, ahead)
+    def _(p):
+        interior(p)
+
     pl.semaphore_wait(barrier, 2 + len(near) + len(far))
 
     sides = ((0, east_dev, cols - H, 0), (1, west_dev, 0, H))
@@ -136,10 +189,10 @@
         )
         c.start()
         tops.append(c)
-    low_state = state_sends(0, slice(0, tags), slice(0, low))
+    low_state = state_sends(0, slice(0, tags), slice(0, low - 1))
     high_winds = wind_sends(1)
     high_state = [
-        state_sends(1 + p, slice(2 * p, 2 * p + 2), slice(low, levels)) for p in range(tags // 2)
+        state_sends(1 + p, slice(2 * p, 2 * p + 2), slice(low - 1, levels)) for p in range(tags // 2)
     ]
 
     def share_part(part):
@@ -148,53 +201,9 @@
             device_id={"grp": twin}, device_id_type=MESH,
         )
 
-    def advance(left, cen, right, c):
-        lv = pl.ds(0, cen.shape[1])
-        north = pltpu.roll(cen, lats - 1, 2)
-        south = pltpu.roll(cen, 1, 2)
-        h = (
-            coef[C0, c, lv][None] * cen
-            + coef[CE, c, lv][None] * right
-            + coef[CW, c, lv][None] * left
-            + coef[CN, c, lv][None] * north
-            + coef[CS, c, lv][None] * south
-        )
-        above = pltpu.roll(h, cen.shape[1] - 1, 1)
-        return h + coef[UP, c, lv][None] * (above - h)
-
-    blank = jnp.zeros((tags, 8, lats), jnp.float32)
-    for c in (H, H + cols - 1):
-        acc[:, c] = blank
-    for n in range(4 * H):
-        edge_acc[:, n] = blank
-
-
-    @pl.loop(0, tags // 2)
+    @pl.loop(ahead, tags // 2)
     def _(p):
-        ks = pl.ds(2 * p, 2)
-
-        def run(c, carry, n, first):
-            old = list(carry) + [state[ks, c + 1 + j] for j in range(n)]
-            for j in range(n):
-                new = advance(old[j], old[j + 1], old[j + 2], c + j)
-                state[ks, c + j] = new
-                if first:
-                    acc[ks, c + j] = new[:, 0:8]
-                else:
-                    acc[ks, c + j] += new[:, 0:8]
-            return old[n], old[n + 1]
-
-        for t in range(1, ITERS + 1):
-            start, size = H + t, cols - 2 * t
-            carry = state[ks, start - 1], state[ks, start]
-            save_l[ks, t - 1] = carry[1]
-            if size % 8:
-                carry = run(start, carry, size % 8, t == 1)
-                start += size % 8
-            carry = lax.fori_loop(
-                0, size // 8, lambda b, v: run(start + 8 * b, v, 8, t == 1), carry
-            )
-            save_r[ks, t - 1] = carry[0]
+        interior(p)
 
     tag0 = grp * tags
     row = lax.broadcasted_iota(jnp.int32, (8, lats), 0)
@@ -287,7 +296,8 @@
             k = 2 * p + j
             ring = turned(
                 jnp.concatenate(
-                    [halo[k, 0:low], jnp.zeros((8 - low, 2 * H, lats), jnp.float32)], axis=0
+                    [halo[k, 0 : low - 1], jnp.zeros((9 - low, 2 * H, lats), jnp.float32)],
+                    axis=0,
                 )
             )
             surf[k, 0:H] = ring[0:H]

time: 34.7 us -> 34.1 us (0.983)
  Pallas kernels: 34 us -> 33.4 us
    pallas_call x1, Pallas kernels: 32.6 us -> 32 us  [local(): pl.pallas_call(kernel, name='adjoint_transport', out_shape=(pltpu.VMEM((t...]
where the time goes in v5:
time: 34.1 us; the launch traced here: 34 us
  Pallas kernels  33.4 us (98%)
  between operations  0.64 us (2%)
    pallas_call x1, Pallas kernels, local(): pl.pallas_call(kernel, name='adjoint_transport', out_shape=(pltpu.VMEM((t...  32 us
    pallas_call x1, Pallas kernels, local(): pl.pallas_call(write_out, name='write_out', out_shape=tuple((jax.ShapeDty...  1.34 us

profile of v5, /device:TPU:1, one launch (start us, length us, event | category | flops | bytes accessed | tf_op | source)
XLA Modules:
  0.0 34.0 jit_solution(42014669177524523)
XLA Ops:
  0.6 32.0 %adjoint_transport.1 = (f32[4,16,32,256]{3,2,1,0:T(8,128)S(1)}, f32[32,256]{1,0:T(8,128)S(1)}) custom-call(f32[4,16,32,256]{3,2,1,0:T(8,128)} %x_ref.1, f32[16,32,256]{2,1,0:T(8,128)} %ew_ref.1, f32[16,32,256]{2,1,0:T(8,128)} %nw_ref.1, f32[16,32,256]{2,1,0:T(8,128)} %ed_ref.1, f32[16,32,256]{2,1,0:T(8,128)} %nd_ref.1, f32[16,32,256]{2,1,0:T(8,128)} %mf_ref.1, ...), custom_call_target="tpu_custom_call" | custom-call | tf_op jit(solution)/shard_map/adjoint_transport/pallas_call | solution.py:412
  32.7 1.3 %write_out.1 = (f32[4,16,32,256]{3,2,1,0:T(8,128)}, f32[32,256]{1,0:T(8,128)}) custom-call(f32[4,16,32,256]{3,2,1,0:T(8,128)S(1)} %get-tuple-element.4.lam_ref, f32[32,256]{1,0:T(8,128)S(1)} %get-tuple-element.5.grad_ref), custom_call_target="tpu_custom_call" | custom-call | tf_op jit(solution)/shard_map/write_out/pallas_call | solution.py:432
